TPU v7x, 32 devices: a whole 2x2x4 slice. The times are simulated.
32 devices in a mesh: members: 2 (over y), lat: 4 (over z), lev: 2 (over x), sub: 2 (over core).
Axes of the slice: x: 2, y: 2, z: 4, core: 2. Of those that a mesh axis runs over, the one named last changes fastest.
Arguments:
- thermal_state_grid: bfloat16 [272, 512, 1024], P(('members', 'lev', 'sub'), 'lat'), parts along dimension 0, may hold values from -6 to 6
- thermal_forcing: bfloat16 [272, 512, 1024], P(('members', 'lev', 'sub'), 'lat'), parts along dimension 0, may hold values from -6 to 6
- spherical_basis_table: bfloat16 [512, 512, 512], P(('lat', 'lev', 'sub')), may hold values from -0.25 to 0.25
- implicit_solver_matrix: bfloat16 [512, 136, 136], P(('lat', 'lev', 'sub')), may hold values from -0.5 to 0.5
- fourier_order_holder: int32 [512], replicated, may hold values from 0 to 511, as said below
Outputs:
- new_temperature: bfloat16 [272, 512, 1024], P(('members', 'lev', 'sub'), 'lat'), parts along dimension 0
There are 2 independent parts, one for each index of `members`. A program takes and returns all parts, laid end to end along the dimension named above; an argument that names none is the same for every part. Nothing has to cross between parts.
Inputs may be any that keep to these rules, and one draw needn't show every extreme that they name: fourier_order_holder is a permutation of the waves; slots 2k and 2k+1 hold waves m and 511-m for some m.
All inputs are finite; a program needn't handle non-finite values.
Results may differ from a plain program's by a relative error of at most 0.0079.
Values may be sent and summed in bfloat16 or wider, within the bound.
A program may use at most 192 MiB of HBM per device.

v0:
```python
import math

import jax
import jax.numpy as jnp
from jax import lax
from jax.sharding import PartitionSpec as P


def raw_table(fourier_order_holder, lon_count):
    meridian_position = jnp.arange(lon_count, dtype=jnp.int32)
    phases = meridian_position[:, None] * fourier_order_holder[None, :] % lon_count
    angles = phases.astype(jnp.float32) * (2.0 * math.pi / lon_count)
    factor = 1.0 / math.sqrt(lon_count)
    stacked = jnp.stack([jnp.cos(angles), -jnp.sin(angles)], axis=2)
    return stacked.reshape(lon_count, 2 * fourier_order_holder.shape[0]) * factor


def shards(
    thermal_state_grid,
    thermal_forcing,
    spherical_basis_table,
    implicit_solver_matrix,
    fourier_order_holder,
):
    layer_group_span, parallel_group_span, meridian_position = thermal_state_grid.shape
    slot_count, lat_total, wave_total = spherical_basis_table.shape
    present_state = thermal_state_grid.astype(jnp.float32)
    explicit = (
        present_state
        + 0.5 * thermal_forcing.astype(jnp.float32)
        - 0.3
        * present_state
        * present_state
        * present_state
        / (1.0 + present_state * present_state)
    ).astype(jnp.bfloat16)
    raw = raw_table(fourier_order_holder, meridian_position)
    analysis = raw.astype(jnp.bfloat16)
    weights = jnp.where(fourier_order_holder == 0, 1.0, 2.0).astype(jnp.float32)
    synthesis = (raw.T * jnp.repeat(weights, 2)[:, None]).astype(jnp.bfloat16)
    spectral = jnp.dot(
        explicit.reshape(layer_group_span * parallel_group_span, meridian_position),
        analysis,
        preferred_element_type=jnp.float32,
    )
    spectral = spectral.astype(jnp.bfloat16).reshape(
        layer_group_span, parallel_group_span, meridian_position
    )
    banded = lax.all_to_all(spectral, "lat", split_axis=2, concat_axis=1, tiled=True)
    gathered = lax.all_gather(spherical_basis_table, ("lev", "sub"), axis=0, tiled=True)
    owner_slots = gathered.shape[0]
    by_slot = banded.reshape(layer_group_span, lat_total, owner_slots, 2)
    part_spec = jnp.einsum(
        "lxsc,sxn->lscn", by_slot, gathered, preferred_element_type=jnp.float32
    ).astype(jnp.bfloat16)
    column = lax.all_to_all(part_spec, ("lev", "sub"), split_axis=1, concat_axis=0, tiled=True)
    solved = jnp.einsum(
        "skl,lscn->kscn", implicit_solver_matrix, column, preferred_element_type=jnp.float32
    )
    owner_index = lax.axis_index(("lat", "lev", "sub"))
    my_waves = lax.dynamic_slice_in_dim(fourier_order_holder, owner_index * slot_count, slot_count)
    degrees = jnp.arange(wave_total, dtype=jnp.int32)
    live_mask = degrees[None, :] >= my_waves[:, None]
    solved = jnp.where(live_mask[None, :, None, :], solved, 0.0).astype(jnp.bfloat16)
    returned = lax.all_to_all(solved, ("lev", "sub"), split_axis=0, concat_axis=1, tiled=True)
    synthesized = jnp.einsum(
        "sxn,lscn->lxsc", gathered, returned, preferred_element_type=jnp.float32
    ).astype(jnp.bfloat16)
    synthesized = synthesized.reshape(layer_group_span, lat_total, 2 * owner_slots)
    grid_spec = lax.all_to_all(synthesized, "lat", split_axis=1, concat_axis=2, tiled=True)
    result = jnp.dot(
        grid_spec.reshape(layer_group_span * parallel_group_span, meridian_position),
        synthesis,
        preferred_element_type=jnp.float32,
    )
    return result.astype(jnp.bfloat16).reshape(
        layer_group_span, parallel_group_span, meridian_position
    )


def solution(mesh):
    return jax.shard_map(
        shards,
        mesh=mesh,
        in_specs=(
            P(("members", "lev", "sub"), "lat", None),
            P(("members", "lev", "sub"), "lat", None),
            P(("lat", "lev", "sub"), None, None),
            P(("lat", "lev", "sub"), None, None),
            P(),
        ),
        out_specs=P(("members", "lev", "sub"), "lat", None),
        check_vma=False,
    )
```

profile of v0, /device:TPU:13, one launch (start us, length us, event | category | flops | bytes accessed | tf_op | source)
XLA Modules:
  0.0 1050.1 jit_solution(9948861162757677807)
XLA Ops:
  6.5 0.7 all-gather.2.cloned.1.call-update
  7.4 8.2 fusion.25
  15.6 4.7 maximum_multiply_fusion
  20.3 7.3 copy.51
  27.6 4.5 convert_element_type.68
  32.1 13.6 %fusion.5 = bf16[34,128,1024]{2,1,0:T(8,128)(2,1)S(1)} fusion(bf16[34,128,1024]{2,1,0:T(8,128)(2,1)} %param.5, bf16[34,128,1024]{2,1,0:T(8,128)(2,1)} %param.6), kind=kLoop, calls=%fused_computation.10 | loop fusion | flops 53477376 | bytes 26738688 | tf_op jit(solution)/shard_map/convert_element_type | solution.py:36
  45.7 11.6 %convolution_convert_fusion.1 = bf16[4352,1024]{1,0:T(8,128)(2,1)} fusion(bf16[4352,1024]{1,0:T(8,128)(2,1)S(1)} %bitcast.63, bf16[1024,1024]{0,1:T(8,128)(2,1)S(1)} %copy-done.2), kind=kOutput, calls=%fused_computation.16 | convolution fusion | flops 9131261952 | bytes 19922944 | tf_op jit(solution)/shard_map/dot_general | solution.py:41
  57.4 15.1 %copy.52 = bf16[34,128,1024]{1,0,2:T(8,128)(2,1)} copy(bf16[34,128,1024]{2,1,0:T(8,128)(2,1)} %bitcast.61) | data formatting | bytes 17825792 | tf_op jit(solution)/shard_map/reshape | solution.py:46
  72.4 230.3 %all_to_all.66 = bf16[34,128,1024]{1,0,2:T(8,128)(2,1)S(1)} all-to-all(bf16[34,128,1024]{1,0,2:T(8,128)(2,1)} %copy.52), channel_id=1, replica_groups=mesh['members'=2,'lat'=4,'lev'=2,'sub'=2] {'lat'}, dimensions={2} | all-to-all | bytes 17825792 | tf_op jit(solution)/shard_map/all_to_all | solution.py:49
  302.7 8.5 copy.70
  311.2 16.5 %reshape.153 = bf16[34,512,128,2]{1,0,3,2:T(8,128)(2,1)} reshape(bf16[34,4,128,256]{2,1,0,3:T(4,128)(2,1)} %copy.70) | data formatting | bytes 17825792 | tf_op jit(solution)/shard_map/reshape | solution.py:52
  327.7 75.5 %all-gather.2.cloned.1.call-done = bf16[128,512,512]{2,1,0:T(8,128)(2,1)} async-done(((bf16[32,512,512]{2,1,0:T(8,128)(2,1)}), bf16[128,512,512]{2,1,0:T(8,128)(2,1)}) %all-gather.2.cloned.1.call-update) | async-done | bytes 67108880 | tf_op jit(solution)/shard_map/all_gather | solution.py:50
  403.2 30.4 %convert_bitcast_fusion = bf16[34,128,2,512]{3,0,2,1:T(8,128)(2,1)} fusion(bf16[34,512,128,2]{1,0,3,2:T(8,128)(2,1)} %reshape.153, bf16[128,512,512]{2,1,0:T(8,128)(2,1)} %all-gather.2.cloned.1.call-done), kind=kOutput, calls=%fused_computation.14 | convolution fusion | flops 4567859200 | bytes 84934656 | tf_op jit(solution)/shard_map/lxsc,sxn->lscn/dot_general | solution.py:53
  433.7 13.8 %copy.56 = bf16[34,128,2,512]{3,2,0,1:T(2,128)(2,1)} copy(bf16[34,128,2,512]{3,0,2,1:T(8,128)(2,1)} %convert_bitcast_fusion) | data formatting | bytes 17825792 | tf_op jit(solution)/shard_map/convert_element_type | solution.py:55
  447.4 6.1 all-to-all-start.1
  453.7 97.8 %all-to-all-done.1 = bf16[34,128,2,512]{3,2,0,1:T(2,128)(2,1)} async-done(((bf16[34,128,2,512]{3,2,0,1:T(2,128)(2,1)}), bf16[34,128,2,512]{3,2,0,1:T(2,128)(2,1)}, u32[]{:S(2)}, u32[]{:S(2)}) %all-to-all-start.1) | async-done | bytes 8912928 | tf_op jit(solution)/shard_map/all_to_all | solution.py:56
  551.5 9.5 copy.57
  561.0 8.8 copy.58
  569.7 16.3 %fusion.14 = bf16[136,32,2,512]{3,0,2,1:T(8,128)(2,1)S(1)} fusion(bf16[136,32,2,512]{3,1,2,0:T(8,128)(2,1)} %bitcast.62, pred[32,512]{1,0:T(8,128)(4,1)S(1)} %iota_compare_fusion, bf16[32,136,136]{2,1,0:T(8,128)(2,1)S(1)} %copy-done), kind=kOutput, calls=%fused_computation.19 | convolution fusion | flops 1221066752 | bytes 19025920 | tf_op jit(solution)/shard_map/skl,lscn->kscn/dot_general | solution.py:57
  586.0 11.6 %copy.60 = bf16[136,32,2,512]{3,2,1,0:T(2,128)(2,1)S(1)} copy(bf16[136,32,2,512]{3,0,2,1:T(8,128)(2,1)S(1)} %fusion.14) | data formatting | bytes 17825792 | tf_op jit(solution)/shard_map/convert_element_type | solution.py:64
  597.6 102.6 %all_to_all.67 = bf16[136,32,2,512]{3,2,1,0:T(2,128)(2,1)} all-to-all(bf16[136,32,2,512]{3,2,1,0:T(2,128)(2,1)S(1)} %copy.60), channel_id=1, replica_groups=mesh['members'=2,'lat'=4,'lev'=2,'sub'=2] {'lev','sub'}, dimensions={0} | all-to-all | bytes 17825792 | tf_op jit(solution)/shard_map/all_to_all | solution.py:65
  700.2 9.8 copy.61
  710.0 12.8 %copy.62 = bf16[34,4,32,2,512]{4,0,3,2,1:T(8,128)(2,1)} copy(bf16[34,4,32,2,512]{4,2,3,0,1:T(8,128)(2,1)} %bitcast.58) | data formatting | bytes 17825792 | tf_op jit(solution)/shard_map/all_to_all | solution.py:65
  722.8 33.8 %fusion.11 = bf16[128,34,2,512]{3,1,2,0:T(8,128)(2,1)} fusion(bf16[34,128,2,512]{3,0,2,1:T(8,128)(2,1)} %bitcast.55, bf16[128,512,512]{2,1,0:T(8,128)(2,1)} %all-gather.2.cloned.1.call-done), kind=kOutput, calls=%fused_computation.18 | convolution fusion | flops 4567859200 | bytes 84934656 | tf_op jit(solution)/shard_map/sxn,lscn->lxsc/dot_general | solution.py:66
  756.6 17.4 %copy.63 = bf16[34,512,256]{2,0,1:T(8,128)(2,1)} copy(bf16[34,512,256]{1,0,2:T(8,128)(2,1)} %bitcast.56) | data formatting | bytes 17825792 | tf_op jit(solution)/shard_map/reshape | solution.py:69
  774.0 6.5 all-to-all-start.3
  780.5 7.3 copy.66
  787.8 6.1 mul.115
  794.2 210.2 %all-to-all-done.3 = bf16[34,512,256]{2,0,1:T(8,128)(2,1)} async-done(((bf16[34,512,256]{2,0,1:T(8,128)(2,1)}), bf16[34,512,256]{2,0,1:T(8,128)(2,1)}, u32[]{:S(2)}, u32[]{:S(2)}) %all-to-all-start.3) | async-done | bytes 8912928 | tf_op jit(solution)/shard_map/all_to_all | solution.py:70
  1004.4 12.9 %copy.65 = bf16[34,128,4,256]{3,2,1,0:T(4,128)(2,1)} copy(bf16[34,128,4,256]{3,0,1,2:T(8,128)(2,1)} %bitcast.21) | data formatting | bytes 17825792 | tf_op jit(solution)/shard_map/all_to_all | solution.py:70
  1017.3 9.9 copy.73
  1027.2 15.6 %convolution_convert_fusion = bf16[4352,1024]{1,0:T(8,128)(2,1)} fusion(bf16[4352,1024]{1,0:T(8,128)(2,1)} %bitcast.60, f32[1024,1024]{0,1:T(8,128)} %mul.115, f32[1024]{0:T(1024)S(1)} %mul.116), kind=kOutput, calls=%fused_computation.15 | convolution fusion | flops 9133359104 | bytes 22024192 | tf_op jit(solution)/shard_map/dot_general | solution.py:71
  (14 shorter events, 0.6 us)
Async XLA Ops:
  6.5 563.2 %copy-start = (bf16[32,136,136]{2,1,0:T(8,128)(2,1)S(1)}, bf16[32,136,136]{2,1,0:T(8,128)(2,1)}, u32[]{:S(2)}) copy-start(bf16[32,136,136]{2,1,0:T(8,128)(2,1)} %param.8) | copy-start | bytes 3551236
  6.5 0.8 copy-start.3
  6.5 396.7 %all-gather.2.cloned.1.call-start = ((), (), s32[]{:S(2)}) async-start(), calls=%async_computation.4 | async-start | bytes 83886080 | tf_op jit(solution)/shard_map/all_gather | solution.py:50
  32.1 13.7 %copy-start.2 = (bf16[1024,1024]{0,1:T(8,128)(2,1)S(1)}, bf16[1024,1024]{0,1:T(8,128)(2,1)}, u32[]{:S(2)}) copy-start(bf16[1024,1024]{0,1:T(8,128)(2,1)} %convert_element_type.68) | copy-start | bytes 6291460
  447.4 104.1 %all-to-all-start.1 = ((bf16[34,128,2,512]{3,2,0,1:T(2,128)(2,1)}), bf16[34,128,2,512]{3,2,0,1:T(2,128)(2,1)}, u32[]{:S(2)}, u32[]{:S(2)}) async-start(bf16[34,128,2,512]{3,2,0,1:T(2,128)(2,1)} %copy.56), calls=%async_computation.1 | async-start | bytes 17825792 | tf_op jit(solution)/shard_map/all_to_all | solution.py:56
  774.0 230.4 %all-to-all-start.3 = ((bf16[34,512,256]{2,0,1:T(8,128)(2,1)}), bf16[34,512,256]{2,0,1:T(8,128)(2,1)}, u32[]{:S(2)}, u32[]{:S(2)}) async-start(bf16[34,512,256]{2,0,1:T(8,128)(2,1)} %copy.63), calls=%async_computation.3 | async-start | bytes 20971520 | tf_op jit(solution)/shard_map/all_to_all | solution.py:70
  1027.2 15.6 %copy-start.1 = (bf16[32,136,136]{2,1,0:T(8,128)(2,1)S(1)}, bf16[32,136,136]{2,1,0:T(8,128)(2,1)}, u32[]{:S(2)}) copy-start(bf16[32,136,136]{2,1,0:T(8,128)(2,1)} %param.8) | copy-start | bytes 3551236
Sparse Core Ops, SparseCore 0:
  8.9 394.2 all-gather.1
where the time goes:
time: 1060 us; the launch traced here: 1050 us
  waiting for transfers between devices  384 us (36%)
  blocking collectives  333 us (31%)
  local copies, waits for them, and re-layouts  172 us (16%)
  matrix products  108 us (10%)
  other arithmetic  26.7 us (3%)
  between operations  13.9 us (1%)
  starting transfers between devices  12.6 us (1%)
    all_to_all x1, blocking collectives, shards(): lax.all_to_all(spectral, 'lat', split_axis=2, concat_axis=1, tiled=True)  230 us
    all_to_all x1, waiting for transfers between devices, shards(): lax.all_to_all(synthesized, 'lat', split_axis=1, concat_axis=2, tiled=True)  210 us
    all_to_all x1, blocking collectives, shards(): lax.all_to_all(solved, ('lev', 'sub'), split_axis=0, concat_axis=1, tiled...  103 us
    all_to_all x1, waiting for transfers between devices, shards(): lax.all_to_all(part_spec, ('lev', 'sub'), split_axis=1, concat_axis=0, ti...  97.8 us
    all_gather x1, waiting for transfers between devices, shards(): lax.all_gather(spherical_basis_table, ('lev', 'sub'), axis=0, tiled=True)  75.5 us
    dot_general x1, matrix products, shards(): jnp.einsum('sxn,lscn->lxsc', gathered, returned, preferred_element_type=j...  33.8 us
    dot_general x1, matrix products, shards(): jnp.einsum('lxsc,sxn->lscn', by_slot, gathered, preferred_element_type=jn...  30.4 us
    reshape x2, local copies, waits for them, and re-layouts, shards(): by_slot = banded.reshape(layer_group_span, lat_total, owner_slots, 2)  25 us
  transfers between devices with their start and end apart: 3, of which 3 were waited for; matrix products, arithmetic and copies ran while one was open for 10% of the time, Pallas kernels for 0%

commit v1 on v0

v1 whole, which is shorter than its diff:
```python
import math

import jax
import jax.numpy as jnp
from jax import lax
from jax.sharding import PartitionSpec as P

CHUNKS = 4
OWNERS = ("lat", "lev", "sub")


def raw_table(waves, lon_count):
    meridian = jnp.arange(lon_count, dtype=jnp.int32)
    phases = waves[:, None] * meridian[None, :] % lon_count
    angles = phases.astype(jnp.float32) * (2.0 * math.pi / lon_count)
    factor = 1.0 / math.sqrt(lon_count)
    return jnp.stack([jnp.cos(angles), -jnp.sin(angles)], axis=1) * factor


def make_shards(lat_parts, level_parts):
    owners = lat_parts * level_parts

    def shards(state, forcing, basis, solver, waves):
        levels, lats, lons = state.shape
        slots, lat_total, degrees = basis.shape
        level_total = solver.shape[1]
        present = state.astype(jnp.float32)
        explicit = (
            present
            + 0.5 * forcing.astype(jnp.float32)
            - 0.3 * present * present * present / (1.0 + present * present)
        ).astype(jnp.bfloat16)
        raw = raw_table(waves, lons)
        analysis = raw.astype(jnp.bfloat16)
        weights = jnp.where(waves == 0, 1.0, 2.0).astype(jnp.float32)
        synthesis = (raw * weights[:, None, None]).astype(jnp.bfloat16)
        chunks = CHUNKS
        part = slots // chunks
        analysis = analysis.reshape(owners, slots, 2, lons)
        synthesis = synthesis.reshape(owners, slots, 2, lons)
        owner = lax.axis_index(OWNERS)
        my_waves = lax.dynamic_slice_in_dim(waves, owner * slots, slots)
        live = jnp.arange(degrees, dtype=jnp.int32)[None, :] >= my_waves[:, None]
        sent = []
        for i in range(chunks):
            own = slice(i * part, (i + 1) * part)
            spectral = jnp.einsum(
                "oscj,lxj->osclx", analysis[:, own], explicit, preferred_element_type=jnp.float32
            ).astype(jnp.bfloat16)
            sent.append(lax.all_to_all(spectral, OWNERS, split_axis=0, concat_axis=0, tiled=True))
        back = []
        for i in range(chunks):
            own = slice(i * part, (i + 1) * part)
            got = sent[i].reshape(lat_parts, level_parts, part, 2, levels, lats)
            table = basis[own]
            columns = got.transpose(2, 3, 1, 4, 0, 5).reshape(part, 2 * level_total, lat_total)
            coeffs = jnp.einsum(
                "srx,sxn->srn", columns, table, preferred_element_type=jnp.float32
            ).astype(jnp.bfloat16).reshape(part, 2, level_total, degrees)
            solved = jnp.einsum(
                "skl,scln->sckn", solver[own], coeffs, preferred_element_type=jnp.float32
            )
            solved = jnp.where(live[own][:, None, None, :], solved, 0.0).astype(jnp.bfloat16)
            grid = jnp.einsum(
                "srn,sxn->srx",
                solved.reshape(part, 2 * level_total, degrees),
                table,
                preferred_element_type=jnp.float32,
            ).astype(jnp.bfloat16)
            grid = grid.reshape(part, 2, level_parts, levels, lat_parts, lats)
            grid = grid.transpose(4, 2, 0, 1, 3, 5).reshape(owners, part, 2, levels, lats)
            back.append(lax.all_to_all(grid, OWNERS, split_axis=0, concat_axis=0, tiled=True))
        waved = jnp.concatenate(back, axis=1)
        result = jnp.einsum(
            "osclx,oscj->lxj", waved, synthesis, preferred_element_type=jnp.float32
        )
        return result.astype(jnp.bfloat16)

    return shards


def solution(mesh):
    lat_parts = mesh.shape["lat"]
    level_parts = mesh.shape["lev"] * mesh.shape["sub"]
    return jax.shard_map(
        make_shards(lat_parts, level_parts),
        mesh=mesh,
        in_specs=(
            P(("members", "lev", "sub"), "lat", None),
            P(("members", "lev", "sub"), "lat", None),
            P(OWNERS, None, None),
            P(OWNERS, None, None),
            P(),
        ),
        out_specs=P(("members", "lev", "sub"), "lat", None),
        check_vma=False,
    )
```

time: 1060 us -> 502 us (0.47)
  blocking collectives: 333 us -> 57.4 us
  waiting for transfers between devices: 384 us -> 206 us
  local copies, waits for them, and re-layouts: 172 us -> 77.7 us
  starting transfers between devices: 12.6 us -> 47.2 us
  matrix products: 108 us -> 82.2 us
  between operations: 13.9 us -> 0.36 us
    all_to_all x2 -> x1, blocking collectives: 333 us -> 57.4 us  [shards(): lax.all_to_all(grid, OWNERS, split_axis=0, concat_axis=0, tiled=True)]
    all_to_all x2 -> x7, waiting for transfers between devices: 308 us -> 206 us  [the longest x4 141 us: shards(): lax.all_to_all(spectral, OWNERS, split_axis=0, concat_axis=0, tiled=True)]
    all_gather x1 -> x0, waiting for transfers between devices: 75.5 us -> none  [shards(): lax.all_gather(spherical_basis_table, ('lev', 'sub'), axis=0, tiled=True)]
    all_to_all x5 -> x0, local copies, waits for them, and re-layouts: 53.7 us -> none  [the longest x2 22.6 us: shards(): lax.all_to_all(solved, ('lev', 'sub'), split_axis=0, concat_axis=1, tiled...]
    convert_element_type x4 -> x0, local copies, waits for them, and re-layouts: 37.1 us -> none  [the longest x1 13.8 us: shards(): part_spec = jnp.einsum('lxsc,sxn->lscn', by_slot, gathered, preferred_ele...]
    all_to_all x2 -> x7, starting transfers between devices: 12.6 us -> 47.2 us  [the longest x4 26.4 us: shards(): lax.all_to_all(spectral, OWNERS, split_axis=0, concat_axis=0, tiled=True)]
    transpose x0 -> x8, local copies, waits for them, and re-layouts: none -> 33.8 us  [the longest x4 17.3 us: shards(): got.transpose(2, 3, 1, 4, 0, 5).reshape(part, 2 * level_total, lat_total)]
    dot_general x5 -> x17, matrix products: 108 us -> 82.2 us  [the longest x4 26.8 us: shards(): jnp.einsum('oscj,lxj->osclx', analysis[:, own], explicit, preferred_eleme...]
  transfers between devices with their start and end apart: 3 -> 7, of which waited for: 3 -> 7; matrix products, arithmetic and copies ran while one was open for 10% -> 27% of each run, Pallas kernels for 0% -> 0%
where the time goes in v1:
time: 502 us; the launch traced here: 492 us
  waiting for transfers between devices  206 us (41%)
  matrix products  82.2 us (16%)
  local copies, waits for them, and re-layouts  77.7 us (15%)
  blocking collectives  57.4 us (11%)
  starting transfers between devices  47.2 us (9%)
  other arithmetic  22 us (4%)
    all_to_all x4, waiting for transfers between devices, shards(): lax.all_to_all(spectral, OWNERS, split_axis=0, concat_axis=0, tiled=True)  141 us
    all_to_all x3, waiting for transfers between devices, shards(): lax.all_to_all(grid, OWNERS, split_axis=0, concat_axis=0, tiled=True)  64.8 us
    all_to_all x1, blocking collectives, shards(): lax.all_to_all(grid, OWNERS, split_axis=0, concat_axis=0, tiled=True)  57.4 us
    dot_general x4, matrix products, shards(): jnp.einsum('oscj,lxj->osclx', analysis[:, own], explicit, preferred_eleme...  26.8 us
    all_to_all x4, starting transfers between devices, shards(): lax.all_to_all(spectral, OWNERS, split_axis=0, concat_axis=0, tiled=True)  26.4 us
    all_to_all x3, starting transfers between devices, shards(): lax.all_to_all(grid, OWNERS, split_axis=0, concat_axis=0, tiled=True)  20.8 us
    reshape x4, local copies, waits for them, and re-layouts, shards(): got.transpose(2, 3, 1, 4, 0, 5).reshape(part, 2 * level_total, lat_total)  18.5 us
    dot_general x4, matrix products, shards(): jnp.einsum('srn,sxn->srx', solved.reshape(part, 2 * level_total, degrees)...  18.3 us
  transfers between devices with their start and end apart: 7, of which 7 were waited for; matrix products, arithmetic and copies ran while one was open for 27% of the time, Pallas kernels for 0%

profile of v1, /device:TPU:13, one launch (start us, length us, event | category | flops | bytes accessed | tf_op | source)
XLA Modules:
  0.0 492.4 jit_solution(15230896179290149125)
XLA Ops:
  1.5 8.3 %fusion.76 = (f32[16,32,1,1024]{3,1,2,0:T(8,128)S(1)}, f32[16,32,1,1024]{3,1,2,0:T(8,128)S(1)}) fusion(s32[16,32]{1,0:T(8,128)S(1)} %mul.102), kind=kLoop, calls=%fused_computation.68 | loop fusion | flops 7864320 | bytes 4196352 | tf_op jit(solution)/shard_map/cos | solution.py:17
  9.9 10.7 %fusion.1 = bf16[34,128,1024]{2,1,0:T(8,128)(2,1)S(1)} fusion(bf16[34,128,1024]{2,1,0:T(8,128)(2,1)} %param.5, bf16[34,128,1024]{2,1,0:T(8,128)(2,1)} %param.6), kind=kLoop, calls=%fused_computation.6 | loop fusion | flops 53477376 | bytes 26738688 | tf_op jit(solution)/shard_map/convert_element_type | solution.py:32
  29.4 6.6 %all-to-all-start.2 = ((bf16[16,8,2,34,128]{4,1,3,2,0:T(8,128)(2,1)}), bf16[16,8,2,34,128]{4,1,3,2,0:T(8,128)(2,1)S(1)}, u32[]{:S(2)}, u32[]{:S(2)}) async-start(bf16[16,8,2,34,128]{4,1,3,2,0:T(8,128)(2,1)} %fusion.43), calls=%async_computation.2 | async-start | bytes 4456448 | tf_op jit(solution)/shard_map/all_to_all | solution.py:50
  36.0 7.6 %fusion.46 = bf16[16,8,2,34,128]{4,1,3,2,0:T(8,128)(2,1)} fusion(bf16[34,128,1024]{2,1,0:T(8,128)(2,1)} %copy-done, bf16[16,32,2,1024]{3,1,2,0:T(8,128)(2,1)} %copy-done.5), kind=kOutput, calls=%fused_computation.58 | convolution fusion | flops 2282815488 | bytes 11665408 | tf_op jit(solution)/shard_map/oscj,lxj->osclx/dot_general | solution.py:47
  43.6 41.0 %all-to-all-done.2 = bf16[16,8,2,34,128]{4,1,3,2,0:T(8,128)(2,1)S(1)} async-done(((bf16[16,8,2,34,128]{4,1,3,2,0:T(8,128)(2,1)}), bf16[16,8,2,34,128]{4,1,3,2,0:T(8,128)(2,1)S(1)}, u32[]{:S(2)}, u32[]{:S(2)}) %all-to-all-start.2) | async-done | bytes 2228256 | tf_op jit(solution)/shard_map/all_to_all | solution.py:50
  86.1 6.5 %all-to-all-start.4 = ((bf16[16,8,2,34,128]{4,1,3,2,0:T(8,128)(2,1)}), bf16[16,8,2,34,128]{4,1,3,2,0:T(8,128)(2,1)S(1)}, u32[]{:S(2)}, u32[]{:S(2)}) async-start(bf16[16,8,2,34,128]{4,1,3,2,0:T(8,128)(2,1)} %fusion.46), calls=%async_computation.4 | async-start | bytes 4456448 | tf_op jit(solution)/shard_map/all_to_all | solution.py:50
  92.6 7.6 %fusion.40 = bf16[16,8,2,34,128]{4,1,3,2,0:T(8,128)(2,1)} fusion(bf16[34,128,1024]{2,1,0:T(8,128)(2,1)} %copy-done, bf16[16,32,2,1024]{3,1,2,0:T(8,128)(2,1)} %copy-done.5), kind=kOutput, calls=%fused_computation.56 | convolution fusion | flops 2282815488 | bytes 11665408 | tf_op jit(solution)/shard_map/oscj,lxj->osclx/dot_general | solution.py:47
  100.2 41.0 %all-to-all-done.4 = bf16[16,8,2,34,128]{4,1,3,2,0:T(8,128)(2,1)S(1)} async-done(((bf16[16,8,2,34,128]{4,1,3,2,0:T(8,128)(2,1)}), bf16[16,8,2,34,128]{4,1,3,2,0:T(8,128)(2,1)S(1)}, u32[]{:S(2)}, u32[]{:S(2)}) %all-to-all-start.4) | async-done | bytes 2228256 | tf_op jit(solution)/shard_map/all_to_all | solution.py:50
  142.6 6.8 %all-to-all-start = ((bf16[16,8,2,34,128]{4,1,3,2,0:T(8,128)(2,1)}), bf16[16,8,2,34,128]{4,1,3,2,0:T(8,128)(2,1)S(1)}, u32[]{:S(2)}, u32[]{:S(2)}) async-start(bf16[16,8,2,34,128]{4,1,3,2,0:T(8,128)(2,1)} %fusion.40), calls=%async_computation | async-start | bytes 4456448 | tf_op jit(solution)/shard_map/all_to_all | solution.py:50
  149.4 7.6 %fusion.49 = bf16[16,8,2,34,128]{4,1,3,2,0:T(8,128)(2,1)} fusion(bf16[34,128,1024]{2,1,0:T(8,128)(2,1)} %copy-done, bf16[16,32,2,1024]{3,1,2,0:T(8,128)(2,1)} %copy-done.5), kind=kOutput, calls=%fused_computation.59 | convolution fusion | flops 2282815488 | bytes 11665408 | tf_op jit(solution)/shard_map/oscj,lxj->osclx/dot_general | solution.py:47
  157.0 40.9 %all-to-all-done = bf16[16,8,2,34,128]{4,1,3,2,0:T(8,128)(2,1)S(1)} async-done(((bf16[16,8,2,34,128]{4,1,3,2,0:T(8,128)(2,1)}), bf16[16,8,2,34,128]{4,1,3,2,0:T(8,128)(2,1)S(1)}, u32[]{:S(2)}, u32[]{:S(2)}) %all-to-all-start) | async-done | bytes 2228256 | tf_op jit(solution)/shard_map/all_to_all | solution.py:50
  199.3 6.5 %all-to-all-start.6 = ((bf16[16,8,2,34,128]{4,1,3,2,0:T(8,128)(2,1)}), bf16[16,8,2,34,128]{4,1,3,2,0:T(8,128)(2,1)S(1)}, u32[]{:S(2)}, u32[]{:S(2)}) async-start(bf16[16,8,2,34,128]{4,1,3,2,0:T(8,128)(2,1)} %fusion.49), calls=%async_computation.6 | async-start | bytes 4456448 | tf_op jit(solution)/shard_map/all_to_all | solution.py:50
  206.7 4.7 copy.17
  211.4 4.9 reshape.178
  222.2 4.9 fusion.61
  227.1 5.0 %reshape.181 = bf16[8,2,4,34,4,128]{5,4,3,2,1,0:T(4,128)(2,1)} reshape(bf16[8,272,512]{2,1,0:T(8,128)(2,1)} %fusion.61) | data formatting | bytes 4456448 | tf_op jit(solution)/shard_map/reshape | solution.py:70
  236.6 17.8 %all-to-all-done.6 = bf16[16,8,2,34,128]{4,1,3,2,0:T(8,128)(2,1)S(1)} async-done(((bf16[16,8,2,34,128]{4,1,3,2,0:T(8,128)(2,1)}), bf16[16,8,2,34,128]{4,1,3,2,0:T(8,128)(2,1)S(1)}, u32[]{:S(2)}, u32[]{:S(2)}) %all-to-all-start.6) | async-done | bytes 2228256 | tf_op jit(solution)/shard_map/all_to_all | solution.py:50
  254.4 6.9 %all-to-all-start.3 = ((bf16[16,8,2,34,128]{4,1,2,3,0:T(8,128)(2,1)}), bf16[16,8,2,34,128]{4,1,2,3,0:T(8,128)(2,1)}, u32[]{:S(2)}, u32[]{:S(2)}) async-start(bf16[16,8,2,34,128]{4,1,2,3,0:T(8,128)(2,1)} %bitcast.118), calls=%async_computation.3 | async-start | bytes 4456448 | tf_op jit(solution)/shard_map/all_to_all | solution.py:72
  266.0 4.8 reshape.184
  276.9 4.9 fusion.67
  281.8 5.0 %reshape.187 = bf16[8,2,4,34,4,128]{5,4,3,2,1,0:T(4,128)(2,1)} reshape(bf16[8,272,512]{2,1,0:T(8,128)(2,1)} %fusion.67) | data formatting | bytes 4456448 | tf_op jit(solution)/shard_map/reshape | solution.py:70
  291.2 18.7 %all-to-all-done.3 = bf16[16,8,2,34,128]{4,1,2,3,0:T(8,128)(2,1)} async-done(((bf16[16,8,2,34,128]{4,1,2,3,0:T(8,128)(2,1)}), bf16[16,8,2,34,128]{4,1,2,3,0:T(8,128)(2,1)}, u32[]{:S(2)}, u32[]{:S(2)}) %all-to-all-start.3) | async-done | bytes 2228256 | tf_op jit(solution)/shard_map/all_to_all | solution.py:72
  309.9 7.1 %all-to-all-start.5 = ((bf16[16,8,2,34,128]{4,1,2,3,0:T(8,128)(2,1)}), bf16[16,8,2,34,128]{4,1,2,3,0:T(8,128)(2,1)}, u32[]{:S(2)}, u32[]{:S(2)}) async-start(bf16[16,8,2,34,128]{4,1,2,3,0:T(8,128)(2,1)} %bitcast.119), calls=%async_computation.5 | async-start | bytes 4456448 | tf_op jit(solution)/shard_map/all_to_all | solution.py:72
  316.9 4.8 copy.15
  321.7 4.9 reshape.172
  332.6 5.0 %fusion.55 = bf16[8,272,512]{2,1,0:T(8,128)(2,1)} fusion(bf16[8,272,512]{2,1,0:T(8,128)(2,1)S(1)} %bitcast.131, bf16[32,512,512]{2,1,0:T(8,128)(2,1)} %param.7), kind=kOutput, calls=%fused_computation.61 | convolution fusion | flops 1141964800 | bytes 8650752 | tf_op jit(solution)/shard_map/srn,sxn->srx/dot_general | solution.py:64
  337.5 5.0 %reshape.175 = bf16[8,2,4,34,4,128]{5,4,3,2,1,0:T(4,128)(2,1)} reshape(bf16[8,272,512]{2,1,0:T(8,128)(2,1)} %fusion.55) | data formatting | bytes 4456448 | tf_op jit(solution)/shard_map/reshape | solution.py:70
  347.0 18.5 %all-to-all-done.5 = bf16[16,8,2,34,128]{4,1,2,3,0:T(8,128)(2,1)} async-done(((bf16[16,8,2,34,128]{4,1,2,3,0:T(8,128)(2,1)}), bf16[16,8,2,34,128]{4,1,2,3,0:T(8,128)(2,1)}, u32[]{:S(2)}, u32[]{:S(2)}) %all-to-all-start.5) | async-done | bytes 2228256 | tf_op jit(solution)/shard_map/all_to_all | solution.py:72
  365.5 6.8 %all-to-all-start.1 = ((bf16[16,8,2,34,128]{4,1,2,3,0:T(8,128)(2,1)}), bf16[16,8,2,34,128]{4,1,2,3,0:T(8,128)(2,1)}, u32[]{:S(2)}, u32[]{:S(2)}) async-start(bf16[16,8,2,34,128]{4,1,2,3,0:T(8,128)(2,1)} %bitcast.117), calls=%async_computation.1 | async-start | bytes 4456448 | tf_op jit(solution)/shard_map/all_to_all | solution.py:72
  393.3 27.6 %all-to-all-done.1 = bf16[16,8,2,34,128]{4,1,2,3,0:T(8,128)(2,1)} async-done(((bf16[16,8,2,34,128]{4,1,2,3,0:T(8,128)(2,1)}), bf16[16,8,2,34,128]{4,1,2,3,0:T(8,128)(2,1)}, u32[]{:S(2)}, u32[]{:S(2)}) %all-to-all-start.1) | async-done | bytes 2228256 | tf_op jit(solution)/shard_map/all_to_all | solution.py:72
  420.9 57.4 %all_to_all.40 = bf16[16,8,2,34,128]{4,1,2,3,0:T(8,128)(2,1)S(1)} all-to-all(bf16[16,8,2,34,128]{4,1,2,3,0:T(8,128)(2,1)S(1)} %bitcast.120), channel_id=1, replica_groups=mesh['members'=2,'lat'=4,'lev'=2,'sub'=2] {'lat','lev','sub'}, dimensions={0} | all-to-all | bytes 4456448 | tf_op jit(solution)/shard_map/all_to_all | solution.py:72
  478.3 13.9 %bitcast_convert_fusion = bf16[34,128,1024]{2,1,0:T(8,128)(2,1)} fusion(bf16[16,32,2,1024,1]{3,1,2,0,4:T(8,128)(2,1)S(1)} %copy-done.4, bf16[16,8,2,34,128]{4,1,2,3,0:T(8,128)(2,1)S(1)} %all_to_all.40, bf16[16,8,2,34,128]{4,1,2,3,0:T(8,128)(2,1)} %all-to-all-done.5, bf16[16,8,2,34,128]{4,1,2,3,0:T(8,128)(2,1)} %all-to-all-done.3, ...), kind=kOutput, calls=%fused_computation.9 | convolution fusion | flops 9166913536 | bytes 19922944 | tf_op jit(solution)/shard_map/osclx,oscj->lxj/dot_general | solution.py:74
  (37 shorter events, 72.4 us)
Async XLA Ops:
  20.6 4.2 copy-start
  22.8 2.7 copy-start.5
  29.4 55.2 %all-to-all-start.2 = ((bf16[16,8,2,34,128]{4,1,3,2,0:T(8,128)(2,1)}), bf16[16,8,2,34,128]{4,1,3,2,0:T(8,128)(2,1)S(1)}, u32[]{:S(2)}, u32[]{:S(2)}) async-start(bf16[16,8,2,34,128]{4,1,3,2,0:T(8,128)(2,1)} %fusion.43), calls=%async_computation.2 | async-start | bytes 4456448 | tf_op jit(solution)/shard_map/all_to_all | solution.py:50
  84.6 1.4 copy-start.3
  86.1 55.1 %all-to-all-start.4 = ((bf16[16,8,2,34,128]{4,1,3,2,0:T(8,128)(2,1)}), bf16[16,8,2,34,128]{4,1,3,2,0:T(8,128)(2,1)S(1)}, u32[]{:S(2)}, u32[]{:S(2)}) async-start(bf16[16,8,2,34,128]{4,1,3,2,0:T(8,128)(2,1)} %fusion.46), calls=%async_computation.4 | async-start | bytes 4456448 | tf_op jit(solution)/shard_map/all_to_all | solution.py:50
  141.2 1.4 copy-start.2
  142.6 55.3 %all-to-all-start = ((bf16[16,8,2,34,128]{4,1,3,2,0:T(8,128)(2,1)}), bf16[16,8,2,34,128]{4,1,3,2,0:T(8,128)(2,1)S(1)}, u32[]{:S(2)}, u32[]{:S(2)}) async-start(bf16[16,8,2,34,128]{4,1,3,2,0:T(8,128)(2,1)} %fusion.40), calls=%async_computation | async-start | bytes 4456448 | tf_op jit(solution)/shard_map/all_to_all | solution.py:50
  197.9 1.4 copy-start.1
  199.3 55.1 %all-to-all-start.6 = ((bf16[16,8,2,34,128]{4,1,3,2,0:T(8,128)(2,1)}), bf16[16,8,2,34,128]{4,1,3,2,0:T(8,128)(2,1)S(1)}, u32[]{:S(2)}, u32[]{:S(2)}) async-start(bf16[16,8,2,34,128]{4,1,3,2,0:T(8,128)(2,1)} %fusion.49), calls=%async_computation.6 | async-start | bytes 4456448 | tf_op jit(solution)/shard_map/all_to_all | solution.py:50
  254.4 55.5 %all-to-all-start.3 = ((bf16[16,8,2,34,128]{4,1,2,3,0:T(8,128)(2,1)}), bf16[16,8,2,34,128]{4,1,2,3,0:T(8,128)(2,1)}, u32[]{:S(2)}, u32[]{:S(2)}) async-start(bf16[16,8,2,34,128]{4,1,2,3,0:T(8,128)(2,1)} %bitcast.118), calls=%async_computation.3 | async-start | bytes 4456448 | tf_op jit(solution)/shard_map/all_to_all | solution.py:72
  309.9 55.6 %all-to-all-start.5 = ((bf16[16,8,2,34,128]{4,1,2,3,0:T(8,128)(2,1)}), bf16[16,8,2,34,128]{4,1,2,3,0:T(8,128)(2,1)}, u32[]{:S(2)}, u32[]{:S(2)}) async-start(bf16[16,8,2,34,128]{4,1,2,3,0:T(8,128)(2,1)} %bitcast.119), calls=%async_computation.5 | async-start | bytes 4456448 | tf_op jit(solution)/shard_map/all_to_all | solution.py:72
  365.5 55.4 %all-to-all-start.1 = ((bf16[16,8,2,34,128]{4,1,2,3,0:T(8,128)(2,1)}), bf16[16,8,2,34,128]{4,1,2,3,0:T(8,128)(2,1)}, u32[]{:S(2)}, u32[]{:S(2)}) async-start(bf16[16,8,2,34,128]{4,1,2,3,0:T(8,128)(2,1)} %bitcast.117), calls=%async_computation.1 | async-start | bytes 4456448 | tf_op jit(solution)/shard_map/all_to_all | solution.py:72
  420.9 57.4 %copy-start.4 = (bf16[16,32,2,1024,1]{3,1,2,0,4:T(8,128)(2,1)S(1)}, bf16[16,32,2,1024,1]{3,1,2,0,4:T(8,128)(2,1)}, u32[]{:S(2)}) copy-start(bf16[16,32,2,1024,1]{3,1,2,0,4:T(8,128)(2,1)} %get-tuple-element.5) | copy-start | bytes 6291460

commit v2 on v1

--- a/solution.py
+++ b/solution.py
@@ -1,11 +1,15 @@
+import functools
 import math
 
 import jax
 import jax.numpy as jnp
 from jax import lax
+from jax.experimental import pallas as pl
+from jax.experimental.pallas import tpu as pltpu
 from jax.sharding import PartitionSpec as P
 
 CHUNKS = 4
+GROUP = 8
 OWNERS = ("lat", "lev", "sub")
 
 
@@ -17,6 +21,264 @@
     return jnp.stack([jnp.cos(angles), -jnp.sin(angles)], axis=1) * factor
 
 
+def place(peer, level_parts):
+    subs = lax.axis_size("sub")
+    return {
+        "lat": peer // level_parts,
+        "lev": (peer % level_parts) // subs,
+        "sub": peer % subs,
+    }
+
+
+def my_place(level_parts):
+    subs = lax.axis_size("sub")
+    return lax.axis_index("lat") * level_parts + lax.axis_index("lev") * subs + lax.axis_index("sub")
+
+
+def exchange(n, level_parts, last, piece, fill, send, out, send_sem, recv_sem, local_sem):
+    mine = my_place(level_parts)
+
+    def copy(peer, landing, cut):
+        return pltpu.make_async_remote_copy(
+            src_ref=send.at[(peer, *cut)],
+            dst_ref=out.at[(landing, *cut)],
+            send_sem=send_sem.at[peer],
+            recv_sem=recv_sem.at[landing],
+            device_id=place(peer, level_parts),
+            device_id_type=pl.DeviceIdType.MESH,
+        )
+
+    def push(d, carry):
+        peer = (mine + d) % n
+        fill(peer)
+        copy(peer, mine, (piece,)).start()
+        return carry
+
+    lax.fori_loop(1, n, push, 0)
+    fill(mine)
+    pltpu.make_async_copy(send.at[mine, piece], out.at[mine, piece], local_sem).start()
+
+    @pl.when(last)
+    def _():
+        def settle(d, carry):
+            peer = (mine + d) % n
+            copy(peer, mine, ()).wait_send()
+            copy(peer, peer, ()).wait_recv()
+            return carry
+
+        lax.fori_loop(1, n, settle, 0)
+        pltpu.make_async_copy(send.at[mine], out.at[mine], local_sem).wait()
+
+
+def greet(n, level_parts):
+    mine = my_place(level_parts)
+    barrier = pltpu.get_barrier_semaphore()
+
+    def hello(d, carry):
+        pl.semaphore_signal(
+            barrier,
+            inc=1,
+            device_id=place((mine + d) % n, level_parts),
+            device_id_type=pl.DeviceIdType.MESH,
+        )
+        return carry
+
+    lax.fori_loop(1, n, hello, 0)
+    pl.semaphore_wait(barrier, n - 1)
+
+
+def dft_kernel(
+    n, level_parts, steps,
+    state, forcing, near, far, out, synthesis, table, send, send_sem, recv_sem, local_sem,
+):
+    step = pl.program_id(0)
+    levels, lats, lons = state.shape
+    tile = near.shape[2]
+
+    def trig(a):
+        return far[0, :, a : a + 1] * near[0] - far[1, :, a : a + 1] * near[1]
+
+    @pl.when(step == 0)
+    def _():
+        for a in range(lons // tile):
+            table[:, a * tile : (a + 1) * tile] = trig(a).astype(jnp.bfloat16)
+        greet(n, level_parts)
+
+    present = state[...].astype(jnp.float32)
+    explicit = (
+        present
+        + 0.5 * forcing[...].astype(jnp.float32)
+        - 0.3 * present * present * present / (1.0 + present * present)
+    ).astype(jnp.bfloat16)
+    spectral = lax.dot_general(
+        table[...],
+        explicit.reshape(levels * lats, lons),
+        (((1,), (1,)), ((), ())),
+        preferred_element_type=jnp.float32,
+    ).astype(jnp.bfloat16)
+    spectral = spectral.reshape(n, -1, levels * lats)
+    for level in range(levels):
+        send[:, step * levels + level] = spectral[:, :, level * lats : (level + 1) * lats]
+
+    @pl.when(step == steps - 1)
+    def _():
+        for a in range(lons // tile):
+            synthesis[:, a * tile : (a + 1) * tile] = (
+                trig(a) * far[2, :, a : a + 1]
+            ).astype(jnp.bfloat16)
+
+    exchange(
+        n, level_parts, step == steps - 1, pl.ds(step * levels, levels), lambda peer: None,
+        send, out, send_sem, recv_sem, local_sem,
+    )
+
+
+def dft_exchange(state, forcing, near, far, n, level_parts):
+    levels, lats, lons = state.shape
+    rows = near.shape[1]
+    few = 2
+    steps = levels // few
+    shape = (n, levels, rows // n, lats)
+    grid_block = pl.BlockSpec((few, lats, lons), lambda i: (i, 0, 0))
+    return pl.pallas_call(
+        functools.partial(dft_kernel, n, level_parts, steps),
+        out_shape=(
+            jax.ShapeDtypeStruct(shape, jnp.bfloat16),
+            jax.ShapeDtypeStruct((rows, lons), jnp.bfloat16),
+        ),
+        grid=(steps,),
+        in_specs=[
+            grid_block,
+            grid_block,
+            pl.BlockSpec(near.shape, lambda i: (0, 0, 0)),
+            pl.BlockSpec(far.shape, lambda i: (0, 0, 0)),
+        ],
+        out_specs=(
+            pl.BlockSpec(memory_space=pl.ANY),
+            pl.BlockSpec((rows, lons), lambda i: (0, 0)),
+        ),
+        scratch_shapes=[
+            pltpu.VMEM((rows, lons), jnp.bfloat16),
+            pltpu.VMEM(shape, jnp.bfloat16),
+            pltpu.SemaphoreType.DMA((n,)),
+            pltpu.SemaphoreType.DMA((n,)),
+            pltpu.SemaphoreType.DMA,
+        ],
+        compiler_params=pltpu.CompilerParams(
+            collective_id=0, has_side_effects=True, vmem_limit_bytes=48 << 20
+        ),
+    )(state, forcing, near, far)
+
+
+def small_tables(waves, lon_count, tile):
+    waves = jnp.repeat(waves, 2)[:, None]
+    quarter = (jnp.arange(waves.shape[0], dtype=jnp.int32) % 2)[:, None] * (lon_count // 4)
+    unit = 2.0 * math.pi / lon_count
+    fine = jnp.arange(tile, dtype=jnp.int32)[None, :] * waves % lon_count
+    coarse = jnp.arange(lon_count // tile, dtype=jnp.int32)[None, :] * tile * waves + quarter
+    fine, coarse = fine.astype(jnp.float32) * unit, (coarse % lon_count).astype(jnp.float32) * unit
+    factor = 1.0 / math.sqrt(lon_count)
+    weights = jnp.broadcast_to(jnp.where(waves == 0, 1.0, 2.0), coarse.shape)
+    near = jnp.stack([jnp.cos(fine), jnp.sin(fine)])
+    far = jnp.stack([jnp.cos(coarse) * factor, jnp.sin(coarse) * factor, weights])
+    return near, far
+
+
+def columns_of_chunk(n, level_parts, levels, lats, got, basis, solver, live, wide, rows, mix, split):
+    lat_parts = n // level_parts
+    total = levels * level_parts
+    pairs = 2 * GROUP
+
+    def gather(q, carry):
+        lanes = pl.ds(pl.multiple_of(q * lats, lats), lats)
+        for g in range(level_parts):
+            wide[g] = got[q * level_parts + g].astype(jnp.float32).reshape(levels * pairs, lats)
+            for k in range(pairs):
+                rows[k, pl.ds(g * levels, levels), lanes] = wide[g, pl.ds(k, levels, stride=pairs), :]
+        return carry
+
+    lax.fori_loop(0, lat_parts, gather, 0)
+
+    def slot(s, carry):
+        table = basis[s]
+        packed = rows[pl.ds(2 * s, 2)].reshape(2 * total, lat_parts * lats).astype(jnp.bfloat16)
+        coeffs = jnp.dot(packed, table, preferred_element_type=jnp.float32)
+        mask = live[s] > 0.5
+        solved = []
+        for c in range(2):
+            part = coeffs[c * total : (c + 1) * total].astype(jnp.bfloat16)
+            part = jnp.dot(solver[s], part, preferred_element_type=jnp.float32)
+            solved.append(jnp.where(mask, part, 0.0))
+        solved = jnp.concatenate(solved, axis=0).astype(jnp.bfloat16)
+        mix[...] = lax.dot_general(
+            solved, table, (((1,), (1,)), ((), ())), preferred_element_type=jnp.float32
+        )
+        for q in range(lat_parts):
+            for g in range(level_parts):
+                for c in range(2):
+                    split[q * level_parts + g, pl.ds(2 * s + c, levels, stride=pairs), :] = mix[
+                        pl.ds(c * total + g * levels, levels), q * lats : (q + 1) * lats
+                    ]
+        return carry
+
+    lax.fori_loop(0, GROUP, slot, 0)
+
+
+def middle_kernel(
+    n, level_parts, levels, lats, steps,
+    got, basis, solver, live, out, wide, rows, mix, split, send, send_sem, recv_sem, local_sem,
+):
+    step = pl.program_id(0)
+
+    @pl.when(step == 0)
+    def _():
+        greet(n, level_parts)
+
+    columns_of_chunk(n, level_parts, levels, lats, got, basis, solver, live, wide, rows, mix, split)
+
+    def fill(peer):
+        send[peer, step] = split[peer].astype(jnp.bfloat16)
+
+    exchange(
+        n, level_parts, step == steps - 1, step, fill,
+        send, out, send_sem, recv_sem, local_sem,
+    )
+
+
+def middle(got, basis, solver, live, n, level_parts):
+    _, levels, _, lats = got.shape
+    slots, lat_total, degrees = basis.shape
+    total = solver.shape[1]
+    pairs = 2 * GROUP
+    steps, span = slots // GROUP, levels * pairs
+    shape = (n, steps, span, lats)
+    return pl.pallas_call(
+        functools.partial(middle_kernel, n, level_parts, levels, lats, steps),
+        out_shape=jax.ShapeDtypeStruct(shape, jnp.bfloat16),
+        grid=(steps,),
+        in_specs=[
+            pl.BlockSpec((n, levels, pairs, lats), lambda i: (0, 0, i, 0)),
+            pl.BlockSpec((GROUP, lat_total, degrees), lambda i: (i, 0, 0)),
+            pl.BlockSpec((GROUP, total, total), lambda i: (i, 0, 0)),
+            pl.BlockSpec((GROUP, 1, degrees), lambda i: (i, 0, 0)),
+        ],
+        out_specs=pl.BlockSpec(memory_space=pl.ANY),
+        scratch_shapes=[
+            pltpu.VMEM((level_parts, span, lats), jnp.float32),
+            pltpu.VMEM((pairs, total, lat_total), jnp.float32),
+            pltpu.VMEM((2 * total, lat_total), jnp.float32),
+            pltpu.VMEM((n, span, lats), jnp.float32),
+            pltpu.VMEM(shape, jnp.bfloat16),
+            pltpu.SemaphoreType.DMA((n,)),
+            pltpu.SemaphoreType.DMA((n,)),
+            pltpu.SemaphoreType.DMA,
+        ],
+        compiler_params=pltpu.CompilerParams(
+            collective_id=1, has_side_effects=True, vmem_limit_bytes=52 << 20
+        ),
+    )(got, basis, solver, live)
+
+
 def make_shards(lat_parts, level_parts):
     owners = lat_parts * level_parts
 
@@ -24,6 +286,20 @@
         levels, lats, lons = state.shape
         slots, lat_total, degrees = basis.shape
         level_total = solver.shape[1]
+        owner = lax.axis_index(OWNERS)
+        my_waves = lax.dynamic_slice_in_dim(waves, owner * slots, slots)
+        live = jnp.arange(degrees, dtype=jnp.int32)[None, :] >= my_waves[:, None]
+        if lats % 128 == 0 and lons % 512 == 0 and slots % GROUP == 0 and levels % 2 == 0:
+            near, far = small_tables(waves, lons, 128)
+            got, synthesis = dft_exchange(state, forcing, near, far, owners, level_parts)
+            alive = live.astype(jnp.float32)[:, None, :]
+            back = middle(got, basis, solver, alive, owners, level_parts)
+            waved = back.reshape(owners, slots // GROUP, levels, 2 * GROUP, lats)
+            synthesis = synthesis.reshape(owners, slots // GROUP, 2 * GROUP, lons)
+            result = jnp.einsum(
+                "ohlkx,ohkj->lxj", waved, synthesis, preferred_element_type=jnp.float32
+            )
+            return result.astype(jnp.bfloat16)
         present = state.astype(jnp.float32)
         explicit = (
             present
@@ -38,9 +314,6 @@
         part = slots // chunks
         analysis = analysis.reshape(owners, slots, 2, lons)
         synthesis = synthesis.reshape(owners, slots, 2, lons)
-        owner = lax.axis_index(OWNERS)
-        my_waves = lax.dynamic_slice_in_dim(waves, owner * slots, slots)
-        live = jnp.arange(degrees, dtype=jnp.int32)[None, :] >= my_waves[:, None]
         sent = []
         for i in range(chunks):
             own = slice(i * part, (i + 1) * part)

time: 502 us -> 430 us (0.86); the launches traced: 492 us -> 429 us
  Pallas kernels: 0 us -> 409 us
  waiting for transfers between devices: 206 us -> 0 us
  local copies, waits for them, and re-layouts: 77.7 us -> 2.19 us
  matrix products: 82.2 us -> 15.1 us
  blocking collectives: 57.4 us -> 0 us
  starting transfers between devices: 47.2 us -> 0 us
  other arithmetic: 22 us -> 2.51 us
    pallas_call x0 -> x2, Pallas kernels: none -> 409 us  [the longest x1 208 us: middle(): pl.pallas_call(functools.partial(middle_kernel, n, level_parts, levels, l...]
    all_to_all x7 -> x0, waiting for transfers between devices: 206 us -> none  [the longest x4 141 us: shards(): lax.all_to_all(spectral, OWNERS, split_axis=0, concat_axis=0, tiled=True)]
    dot_general x17 -> x1, matrix products: 82.2 us -> 15.1 us  [shards(): jnp.einsum('ohlkx,ohkj->lxj', waved, synthesis, preferred_element_type=jn...]
    all_to_all x1 -> x0, blocking collectives: 57.4 us -> none  [shards(): lax.all_to_all(grid, OWNERS, split_axis=0, concat_axis=0, tiled=True)]
    all_to_all x7 -> x0, starting transfers between devices: 47.2 us -> none  [the longest x4 26.4 us: shards(): lax.all_to_all(spectral, OWNERS, split_axis=0, concat_axis=0, tiled=True)]
    reshape x8 -> x0, local copies, waits for them, and re-layouts: 35.5 us -> none  [the longest x4 18.5 us: shards(): got.transpose(2, 3, 1, 4, 0, 5).reshape(part, 2 * level_total, lat_total)]
    transpose x8 -> x0, local copies, waits for them, and re-layouts: 33.8 us -> none  [the longest x4 17.3 us: shards(): got.transpose(2, 3, 1, 4, 0, 5).reshape(part, 2 * level_total, lat_total)]
    convert_element_type x2 -> x1, other arithmetic: 12.9 us -> 0.1 us  [shards(): alive = live.astype(jnp.float32)[:, None, :]]
  transfers between devices with their start and end apart: 7 -> 0, of which waited for: 7 -> 0; matrix products, arithmetic and copies ran while one was open for 27% -> 0% of each run, Pallas kernels for 0% -> 0%
where the time goes in v2:
time: 430 us; the launch traced here: 429 us
  Pallas kernels  409 us (95%)
  matrix products  15.1 us (4%)
    pallas_call x1, Pallas kernels, middle(): pl.pallas_call(functools.partial(middle_kernel, n, level_parts, levels, l...  208 us
    pallas_call x1, Pallas kernels, dft_exchange(): pl.pallas_call(functools.partial(dft_kernel, n, level_parts, steps), out_...  201 us
    dot_general x1, matrix products, shards(): jnp.einsum('ohlkx,ohkj->lxj', waved, synthesis, preferred_element_type=jn...  15.1 us

profile of v2, /device:TPU:13, one launch (start us, length us, event | category | flops | bytes accessed | tf_op | source)
XLA Modules:
  0.0 428.7 jit_solution(7486042149386906185)
XLA Ops:
  0.0 0.8 dynamic_slice.3
  0.8 0.1 compare_convert_fusion.live
  0.9 0.8 broadcast_in_dim.10
  1.7 0.2 mul.133
  1.9 0.2 cosine_multiply_fusion
  2.1 2.1 fusion.12
  4.2 0.1 pad_maximum_fusion.near
  4.3 0.5 copy.10.far
  4.8 200.8 %shard_map.55 = (bf16[16,34,64,128]{3,2,1,0:T(8,128)(2,1)}, bf16[1024,1024]{1,0:T(8,128)(2,1)S(1)}) custom-call(bf16[34,128,1024]{2,1,0:T(8,128)(2,1)} %state.1, bf16[34,128,1024]{2,1,0:T(8,128)(2,1)} %forcing.1, f32[2,1024,128]{2,1,0:T(8,128)S(1)} %pad_maximum_fusion.near, f32[3,1024,8]{2,1,0:T(8,128)S(1)} %copy.10.far), custom_call_target="tpu_custom_call" | custom-call | tf_op jit(solution)/shard_map/pallas_call | solution.py:143
  205.6 207.9 %shard_map.56 = bf16[16,4,544,128]{3,2,1,0:T(8,128)(2,1)} custom-call(bf16[16,34,64,128]{3,2,1,0:T(8,128)(2,1)} %get-tuple-element.7.got, bf16[32,512,512]{2,1,0:T(8,128)(2,1)} %basis.1, bf16[32,136,136]{2,1,0:T(8,128)(2,1)} %solver.1, f32[32,1,512]{2,1,0:T(1,128)S(1)} %compare_convert_fusion.live), custom_call_target="tpu_custom_call" | custom-call | tf_op jit(solution)/shard_map/pallas_call | solution.py:255
  413.5 15.1 %bitcast_convert_fusion = bf16[34,128,1024]{2,1,0:T(8,128)(2,1)} fusion(bf16[16,4,34,16,128]{4,3,2,1,0:T(8,128)(2,1)} %bitcast.9, bf16[16,4,16,1024,1]{3,2,1,0,4:T(8,128)(2,1)S(1)} %bitcast.8), kind=kOutput, calls=%fused_computation | convolution fusion | flops 9131261952 | bytes 19922944 | tf_op jit(solution)/shard_map/ohlkx,ohkj->lxj/dot_general | solution.py:299
  (5 shorter events, 0.0 us)

commit v3 on v2

--- a/solution.py
+++ b/solution.py
@@ -48,14 +48,21 @@
             device_id_type=pl.DeviceIdType.MESH,
         )
 
-    def push(d, carry):
-        peer = (mine + d) % n
+    lat_parts = n // level_parts
+    lat, group, sub = mine // level_parts, mine % level_parts, lax.axis_index("sub")
+
+    def push(t, carry):
+        turn = (lat + t // level_parts + (1 - sub) * (lat_parts // 2)) % lat_parts
+        peer = turn * level_parts + (group + t) % level_parts
         fill(peer)
-        copy(peer, mine, (piece,)).start()
+
+        @pl.when(peer != mine)
+        def _():
+            copy(peer, mine, (piece,)).start()
+
         return carry
 
-    lax.fori_loop(1, n, push, 0)
-    fill(mine)
+    lax.fori_loop(0, n, push, 0)
     pltpu.make_async_copy(send.at[mine, piece], out.at[mine, piece], local_sem).start()
 
     @pl.when(last)
@@ -84,7 +91,6 @@
         return carry
 
     lax.fori_loop(1, n, hello, 0)
-    pl.semaphore_wait(barrier, n - 1)
 
 
 def dft_kernel(
@@ -100,9 +106,9 @@
 
     @pl.when(step == 0)
     def _():
+        greet(n, level_parts)
         for a in range(lons // tile):
             table[:, a * tile : (a + 1) * tile] = trig(a).astype(jnp.bfloat16)
-        greet(n, level_parts)
 
     present = state[...].astype(jnp.float32)
     explicit = (
@@ -116,6 +122,11 @@
         (((1,), (1,)), ((), ())),
         preferred_element_type=jnp.float32,
     ).astype(jnp.bfloat16)
+
+    @pl.when(step == 0)
+    def _():
+        pl.semaphore_wait(pltpu.get_barrier_semaphore(), n - 1)
+
     spectral = spectral.reshape(n, -1, levels * lats)
     for level in range(levels):
         send[:, step * levels + level] = spectral[:, :, level * lats : (level + 1) * lats]
@@ -235,6 +246,10 @@
         greet(n, level_parts)
 
     columns_of_chunk(n, level_parts, levels, lats, got, basis, solver, live, wide, rows, mix, split)
+
+    @pl.when(step == 0)
+    def _():
+        pl.semaphore_wait(pltpu.get_barrier_semaphore(), n - 1)
 
     def fill(peer):
         send[peer, step] = split[peer].astype(jnp.bfloat16)

time: 430 us -> 426 us (level)
  no operation moved by 1% of the time
where the time goes in v3:
time: 426 us; the launch traced here: 425 us
  Pallas kernels  405 us (95%)
  matrix products  15.1 us (4%)
    pallas_call x1, Pallas kernels, middle(): pl.pallas_call(functools.partial(middle_kernel, n, level_parts, levels, l...  206 us
    pallas_call x1, Pallas kernels, dft_exchange(): pl.pallas_call(functools.partial(dft_kernel, n, level_parts, steps), out_...  200 us
    dot_general x1, matrix products, shards(): jnp.einsum('ohlkx,ohkj->lxj', waved, synthesis, preferred_element_type=jn...  15.1 us

profile of v3, /device:TPU:13, one launch (start us, length us, event | category | flops | bytes accessed | tf_op | source)
XLA Modules:
  0.0 425.4 jit_solution(11234315181159615746)
XLA Ops:
  0.0 0.8 dynamic_slice.3
  0.8 0.1 compare_convert_fusion.live
  0.9 0.8 broadcast_in_dim.10
  1.7 0.2 mul.133
  1.9 0.2 cosine_multiply_fusion
  2.1 2.1 fusion.12
  4.2 0.1 pad_maximum_fusion.near
  4.3 0.5 copy.10.far
  4.8 199.9 %shard_map.55 = (bf16[16,34,64,128]{3,2,1,0:T(8,128)(2,1)}, bf16[1024,1024]{1,0:T(8,128)(2,1)S(1)}) custom-call(bf16[34,128,1024]{2,1,0:T(8,128)(2,1)} %state.1, bf16[34,128,1024]{2,1,0:T(8,128)(2,1)} %forcing.1, f32[2,1024,128]{2,1,0:T(8,128)S(1)} %pad_maximum_fusion.near, f32[3,1024,8]{2,1,0:T(8,128)S(1)} %copy.10.far), custom_call_target="tpu_custom_call" | custom-call | tf_op jit(solution)/shard_map/pallas_call | solution.py:154
  204.7 205.5 %shard_map.56 = bf16[16,4,544,128]{3,2,1,0:T(8,128)(2,1)} custom-call(bf16[16,34,64,128]{3,2,1,0:T(8,128)(2,1)} %get-tuple-element.7.got, bf16[32,512,512]{2,1,0:T(8,128)(2,1)} %basis.1, bf16[32,136,136]{2,1,0:T(8,128)(2,1)} %solver.1, f32[32,1,512]{2,1,0:T(1,128)S(1)} %compare_convert_fusion.live), custom_call_target="tpu_custom_call" | custom-call | tf_op jit(solution)/shard_map/pallas_call | solution.py:270
  410.2 15.1 %bitcast_convert_fusion = bf16[34,128,1024]{2,1,0:T(8,128)(2,1)} fusion(bf16[16,4,34,16,128]{4,3,2,1,0:T(8,128)(2,1)} %bitcast.9, bf16[16,4,16,1024,1]{3,2,1,0,4:T(8,128)(2,1)S(1)} %bitcast.8), kind=kOutput, calls=%fused_computation | convolution fusion | flops 9131261952 | bytes 19922944 | tf_op jit(solution)/shard_map/ohlkx,ohkj->lxj/dot_general | solution.py:314
  (5 shorter events, 0.0 us)
